TPU v7x, 256 devices: a whole 4x4x8 slice. The times are simulated.
256 devices in a mesh: feat: 8 (over x, core), rows: 32 (over z, y).
Axes of the slice: x: 4, y: 4, z: 8, core: 2. Of those that a mesh axis runs over, the one named last changes fastest.
Arguments:
- features: bfloat16 [65536, 8192], P('rows', 'feat'), may hold values from -6 to 6
- residual: float32 [65536, 1024], P('rows', 'feat'), may hold values from -8 to 8
- inverse_grams: float32 [8192, 1024], P('feat'), may hold values from -1 to 1, as said below
Outputs:
- increments: bfloat16 [1024, 8192], P(None, 'feat')
- final_residual: float32 [65536, 1024], P('rows', 'feat')
Inputs may be any that keep to these rules, and one draw needn't show every extreme that they name: `inverse_grams`: each block of 1024 rows is a symmetric positive definite matrix.
All inputs are finite; a program needn't handle non-finite values.
Results may differ from a plain program's by a relative error of at most 0.0051.
Values may be sent and summed in bfloat16 or wider, within the bound.
A program may use at most 64 MiB of HBM per device.

v0:
```python
import jax
import jax.numpy as jnp
from jax import lax
from jax.sharding import PartitionSpec as P


def from_behind(value, axis, steps):
    count = lax.axis_size(axis)
    pairs = [(source, (source + steps) % count) for source in range(count)]
    return lax.ppermute(value, axis, pairs)


def on_device(features, residual, inverse_grams):
    block_total = lax.axis_size("feat")
    block_id = lax.axis_index("feat")
    piece_width = residual.shape[1]
    feat_width = features.shape[1]
    contract_rows = (((0,), (0,)), ((), ()))
    contract_cols = (((1,), (1,)), ((), ()))
    start_incr = jnp.zeros((piece_width * block_total, feat_width), jnp.bfloat16)

    def advance(visit, state_pair):
        current, increments = state_pair
        front_index = (block_id - visit) % block_total
        rounded = current.astype(jnp.bfloat16)
        partial_value = lax.dot_general(
            rounded, features, contract_rows, preferred_element_type=jnp.float32
        )
        summed_term = lax.psum(partial_value, "rows")
        update = lax.dot_general(
            summed_term, inverse_grams, contract_cols, precision=lax.Precision.HIGHEST
        ).astype(jnp.bfloat16)
        current = current - lax.dot_general(
            features, update, contract_cols, preferred_element_type=jnp.float32
        )
        increments = lax.dynamic_update_slice_in_dim(
            increments, update, front_index * piece_width, 0
        )
        current = from_behind(current, "feat", 1)
        return (current, increments)

    final_current, increments = lax.fori_loop(0, block_total, advance, (residual, start_incr))
    return (increments, final_current)


def solution(mesh):
    placed = (P("rows", "feat"), P("rows", "feat"), P("feat", None))
    return jax.shard_map(
        on_device,
        mesh=mesh,
        in_specs=placed,
        out_specs=(P(None, "feat"), P("rows", "feat")),
        check_vma=False,
    )
```

profile of v0, /device:TPU:2, one launch (start us, length us, event | category | flops | bytes accessed | tf_op | source)
XLA Modules:
  0.0 1415.3 jit_solution(5744996908963075979)
XLA Ops:
  7.2 1.6 copy.5
  8.7 1.6 broadcast_in_dim.3
  10.3 1396.8 %while.17 = (s32[]{:T(128)}, f32[2048,128]{0,1:T(8,128)S(1)}, bf16[1024,1024]{1,0:T(8,128)(2,1)}, bf16[2048,1024]{1,0:T(8,128)(2,1)}, f32[1024,1024]{1,0:T(8,128...) while((s32[]{:T(128)}, f32[2048,128]{0,1:T(8,128)S(1)}, ...), condition=%wide.region_2.3_spmd, body=%wide.region_0.2_spmd.sunk | while | flops 2685140992 | bytes 41681292 | solution.py:42
  10.3 0.0 all-reduce.2.cloned.1.call-start
  10.3 3.7 fusion.22
  14.0 0.0 all-reduce.2.cloned.1.call-update
  14.1 152.9 %all-reduce.2.cloned.1.call-done = f32[128,1024]{1,0:T(8,128)} async-done(((f32[128,1024]{1,0:T(8,128)}), f32[128,1024]{1,0:T(8,128)}) %all-reduce.2.cloned.1.call-update) | async-done | bytes 524304 | tf_op jit(solution)/shard_map/while/body/eval_jaxpr/psum | solution.py:29
  166.9 7.6 constant_dynamic-update-slice_fusion.2
  174.5 0.0 copy-done
  174.5 1.5 fusion.23
  176.1 0.0 collective-permute-start
  176.1 14.2 %collective-permute-done = f32[2048,128]{0,1:T(8,128)S(1)} collective-permute-done((f32[2048,128]{0,1:T(8,128)S(1)}, f32[2048,128]{0,1:T(8,128)S(1)}, u32[]{:S(2)}, u32[]{:S(2)}) %collective-permute-start) | collective-permute-done | bytes 1048608 | tf_op jit(solution)/shard_map/while/body/eval_jaxpr/ppermute | solution.py:10
  190.3 3.7 fusion.22
  194.0 0.0 all-reduce.2.cloned.1.call-update
  194.0 146.9 %all-reduce.2.cloned.1.call-done = f32[128,1024]{1,0:T(8,128)} async-done(((f32[128,1024]{1,0:T(8,128)}), f32[128,1024]{1,0:T(8,128)}) %all-reduce.2.cloned.1.call-update) | async-done | bytes 524304 | tf_op jit(solution)/shard_map/while/body/eval_jaxpr/psum | solution.py:29
  340.9 7.6 constant_dynamic-update-slice_fusion.2
  348.5 1.5 fusion.23
  350.0 0.0 collective-permute-start
  350.1 14.2 %collective-permute-done = f32[2048,128]{0,1:T(8,128)S(1)} collective-permute-done((f32[2048,128]{0,1:T(8,128)S(1)}, f32[2048,128]{0,1:T(8,128)S(1)}, u32[]{:S(2)}, u32[]{:S(2)}) %collective-permute-start) | collective-permute-done | bytes 1048608 | tf_op jit(solution)/shard_map/while/body/eval_jaxpr/ppermute | solution.py:10
  364.3 3.7 fusion.22
  368.0 0.0 all-reduce.2.cloned.1.call-update
  368.0 146.8 %all-reduce.2.cloned.1.call-done = f32[128,1024]{1,0:T(8,128)} async-done(((f32[128,1024]{1,0:T(8,128)}), f32[128,1024]{1,0:T(8,128)}) %all-reduce.2.cloned.1.call-update) | async-done | bytes 524304 | tf_op jit(solution)/shard_map/while/body/eval_jaxpr/psum | solution.py:29
  514.9 7.6 constant_dynamic-update-slice_fusion.2
  522.4 1.5 fusion.23
  524.0 0.0 collective-permute-start
  524.0 14.2 %collective-permute-done = f32[2048,128]{0,1:T(8,128)S(1)} collective-permute-done((f32[2048,128]{0,1:T(8,128)S(1)}, f32[2048,128]{0,1:T(8,128)S(1)}, u32[]{:S(2)}, u32[]{:S(2)}) %collective-permute-start) | collective-permute-done | bytes 1048608 | tf_op jit(solution)/shard_map/while/body/eval_jaxpr/ppermute | solution.py:10
  538.2 3.7 fusion.22
  541.9 0.0 all-reduce.2.cloned.1.call-update
  542.0 146.5 %all-reduce.2.cloned.1.call-done = f32[128,1024]{1,0:T(8,128)} async-done(((f32[128,1024]{1,0:T(8,128)}), f32[128,1024]{1,0:T(8,128)}) %all-reduce.2.cloned.1.call-update) | async-done | bytes 524304 | tf_op jit(solution)/shard_map/while/body/eval_jaxpr/psum | solution.py:29
  688.5 7.6 constant_dynamic-update-slice_fusion.2
  696.1 1.5 fusion.23
  697.6 0.0 collective-permute-start
  697.7 14.2 %collective-permute-done = f32[2048,128]{0,1:T(8,128)S(1)} collective-permute-done((f32[2048,128]{0,1:T(8,128)S(1)}, f32[2048,128]{0,1:T(8,128)S(1)}, u32[]{:S(2)}, u32[]{:S(2)}) %collective-permute-start) | collective-permute-done | bytes 1048608 | tf_op jit(solution)/shard_map/while/body/eval_jaxpr/ppermute | solution.py:10
  711.9 0.0 all-reduce.2.cloned.1.call-start
  711.9 3.7 fusion.22
  715.6 0.0 all-reduce.2.cloned.1.call-update
  715.6 146.6 %all-reduce.2.cloned.1.call-done = f32[128,1024]{1,0:T(8,128)} async-done(((f32[128,1024]{1,0:T(8,128)}), f32[128,1024]{1,0:T(8,128)}) %all-reduce.2.cloned.1.call-update) | async-done | bytes 524304 | tf_op jit(solution)/shard_map/while/body/eval_jaxpr/psum | solution.py:29
  862.2 7.6 constant_dynamic-update-slice_fusion.2
  869.8 1.5 fusion.23
  871.3 0.0 collective-permute-start
  871.3 14.2 %collective-permute-done = f32[2048,128]{0,1:T(8,128)S(1)} collective-permute-done((f32[2048,128]{0,1:T(8,128)S(1)}, f32[2048,128]{0,1:T(8,128)S(1)}, u32[]{:S(2)}, u32[]{:S(2)}) %collective-permute-start) | collective-permute-done | bytes 1048608 | tf_op jit(solution)/shard_map/while/body/eval_jaxpr/ppermute | solution.py:10
  885.5 3.7 fusion.22
  889.2 0.0 all-reduce.2.cloned.1.call-update
  889.3 146.6 %all-reduce.2.cloned.1.call-done = f32[128,1024]{1,0:T(8,128)} async-done(((f32[128,1024]{1,0:T(8,128)}), f32[128,1024]{1,0:T(8,128)}) %all-reduce.2.cloned.1.call-update) | async-done | bytes 524304 | tf_op jit(solution)/shard_map/while/body/eval_jaxpr/psum | solution.py:29
  1035.8 7.6 constant_dynamic-update-slice_fusion.2
  1043.4 1.5 fusion.23
  1045.0 0.0 collective-permute-start
  1045.0 14.2 %collective-permute-done = f32[2048,128]{0,1:T(8,128)S(1)} collective-permute-done((f32[2048,128]{0,1:T(8,128)S(1)}, f32[2048,128]{0,1:T(8,128)S(1)}, u32[]{:S(2)}, u32[]{:S(2)}) %collective-permute-start) | collective-permute-done | bytes 1048608 | tf_op jit(solution)/shard_map/while/body/eval_jaxpr/ppermute | solution.py:10
  1059.2 3.7 fusion.22
  1062.9 0.0 all-reduce.2.cloned.1.call-update
  1063.0 146.9 %all-reduce.2.cloned.1.call-done = f32[128,1024]{1,0:T(8,128)} async-done(((f32[128,1024]{1,0:T(8,128)}), f32[128,1024]{1,0:T(8,128)}) %all-reduce.2.cloned.1.call-update) | async-done | bytes 524304 | tf_op jit(solution)/shard_map/while/body/eval_jaxpr/psum | solution.py:29
  1209.8 7.6 constant_dynamic-update-slice_fusion.2
  1217.4 0.0 copy-done
  1217.4 1.5 fusion.23
  1218.9 0.0 collective-permute-start
  1219.0 14.2 %collective-permute-done = f32[2048,128]{0,1:T(8,128)S(1)} collective-permute-done((f32[2048,128]{0,1:T(8,128)S(1)}, f32[2048,128]{0,1:T(8,128)S(1)}, u32[]{:S(2)}, u32[]{:S(2)}) %collective-permute-start) | collective-permute-done | bytes 1048608 | tf_op jit(solution)/shard_map/while/body/eval_jaxpr/ppermute | solution.py:10
  1233.2 3.7 fusion.22
  1236.9 0.0 all-reduce.2.cloned.1.call-update
  1236.9 146.9 %all-reduce.2.cloned.1.call-done = f32[128,1024]{1,0:T(8,128)} async-done(((f32[128,1024]{1,0:T(8,128)}), f32[128,1024]{1,0:T(8,128)}) %all-reduce.2.cloned.1.call-update) | async-done | bytes 524304 | tf_op jit(solution)/shard_map/while/body/eval_jaxpr/psum | solution.py:29
  1383.8 7.6 constant_dynamic-update-slice_fusion.2
  1391.4 1.5 fusion.23
  1392.9 0.0 collective-permute-start
  1392.9 14.2 %collective-permute-done = f32[2048,128]{0,1:T(8,128)S(1)} collective-permute-done((f32[2048,128]{0,1:T(8,128)S(1)}, f32[2048,128]{0,1:T(8,128)S(1)}, u32[]{:S(2)}, u32[]{:S(2)}) %collective-permute-start) | collective-permute-done | bytes 1048608 | tf_op jit(solution)/shard_map/while/body/eval_jaxpr/ppermute | solution.py:10
  1407.2 1.3 copy.6
  (20 shorter events, 0.0 us)
Async XLA Ops:
  10.3 156.6 %all-reduce.2.cloned.1.call-start = ((), (), s32[]{:S(2)}) async-start(), calls=%async_computation | async-start | bytes 1048576 | tf_op jit(solution)/shard_map/while/body/eval_jaxpr/psum | solution.py:29
  166.9 7.6 copy-start
  176.1 14.2 %collective-permute-start = (f32[2048,128]{0,1:T(8,128)S(1)}, f32[2048,128]{0,1:T(8,128)S(1)}, u32[]{:S(2)}, u32[]{:S(2)}) collective-permute-start(f32[2048,128]{0,1:T(8,128)S(1)} %fusion.23), channel_id=1, source_target_pairs={{0,32},{32,64},{64,96},{96,128},{128,160},{160,192},{192,224},{224... | collective-permute-start | bytes 3145736 | tf_op jit(solution)/shard_map/while/body/eval_jaxpr/ppermute | solution.py:10
  190.3 150.6 %all-reduce.2.cloned.1.call-start = ((), (), s32[]{:S(2)}) async-start(), calls=%async_computation | async-start | bytes 1048576 | tf_op jit(solution)/shard_map/while/body/eval_jaxpr/psum | solution.py:29
  340.9 7.6 copy-start
  350.0 14.2 %collective-permute-start = (f32[2048,128]{0,1:T(8,128)S(1)}, f32[2048,128]{0,1:T(8,128)S(1)}, u32[]{:S(2)}, u32[]{:S(2)}) collective-permute-start(f32[2048,128]{0,1:T(8,128)S(1)} %fusion.23), channel_id=1, source_target_pairs={{0,32},{32,64},{64,96},{96,128},{128,160},{160,192},{192,224},{224... | collective-permute-start | bytes 3145736 | tf_op jit(solution)/shard_map/while/body/eval_jaxpr/ppermute | solution.py:10
  364.3 150.6 %all-reduce.2.cloned.1.call-start = ((), (), s32[]{:S(2)}) async-start(), calls=%async_computation | async-start | bytes 1048576 | tf_op jit(solution)/shard_map/while/body/eval_jaxpr/psum | solution.py:29
  514.9 7.6 copy-start
  524.0 14.2 %collective-permute-start = (f32[2048,128]{0,1:T(8,128)S(1)}, f32[2048,128]{0,1:T(8,128)S(1)}, u32[]{:S(2)}, u32[]{:S(2)}) collective-permute-start(f32[2048,128]{0,1:T(8,128)S(1)} %fusion.23), channel_id=1, source_target_pairs={{0,32},{32,64},{64,96},{96,128},{128,160},{160,192},{192,224},{224... | collective-permute-start | bytes 3145736 | tf_op jit(solution)/shard_map/while/body/eval_jaxpr/ppermute | solution.py:10
  538.2 150.3 %all-reduce.2.cloned.1.call-start = ((), (), s32[]{:S(2)}) async-start(), calls=%async_computation | async-start | bytes 1048576 | tf_op jit(solution)/shard_map/while/body/eval_jaxpr/psum | solution.py:29
  688.5 7.6 copy-start
  697.6 14.2 %collective-permute-start = (f32[2048,128]{0,1:T(8,128)S(1)}, f32[2048,128]{0,1:T(8,128)S(1)}, u32[]{:S(2)}, u32[]{:S(2)}) collective-permute-start(f32[2048,128]{0,1:T(8,128)S(1)} %fusion.23), channel_id=1, source_target_pairs={{0,32},{32,64},{64,96},{96,128},{128,160},{160,192},{192,224},{224... | collective-permute-start | bytes 3145736 | tf_op jit(solution)/shard_map/while/body/eval_jaxpr/ppermute | solution.py:10
  711.9 150.3 %all-reduce.2.cloned.1.call-start = ((), (), s32[]{:S(2)}) async-start(), calls=%async_computation | async-start | bytes 1048576 | tf_op jit(solution)/shard_map/while/body/eval_jaxpr/psum | solution.py:29
  862.2 7.6 copy-start
  871.3 14.2 %collective-permute-start = (f32[2048,128]{0,1:T(8,128)S(1)}, f32[2048,128]{0,1:T(8,128)S(1)}, u32[]{:S(2)}, u32[]{:S(2)}) collective-permute-start(f32[2048,128]{0,1:T(8,128)S(1)} %fusion.23), channel_id=1, source_target_pairs={{0,32},{32,64},{64,96},{96,128},{128,160},{160,192},{192,224},{224... | collective-permute-start | bytes 3145736 | tf_op jit(solution)/shard_map/while/body/eval_jaxpr/ppermute | solution.py:10
  885.5 150.3 %all-reduce.2.cloned.1.call-start = ((), (), s32[]{:S(2)}) async-start(), calls=%async_computation | async-start | bytes 1048576 | tf_op jit(solution)/shard_map/while/body/eval_jaxpr/psum | solution.py:29
  1035.8 7.6 copy-start
  1045.0 14.2 %collective-permute-start = (f32[2048,128]{0,1:T(8,128)S(1)}, f32[2048,128]{0,1:T(8,128)S(1)}, u32[]{:S(2)}, u32[]{:S(2)}) collective-permute-start(f32[2048,128]{0,1:T(8,128)S(1)} %fusion.23), channel_id=1, source_target_pairs={{0,32},{32,64},{64,96},{96,128},{128,160},{160,192},{192,224},{224... | collective-permute-start | bytes 3145736 | tf_op jit(solution)/shard_map/while/body/eval_jaxpr/ppermute | solution.py:10
  1059.2 150.6 %all-reduce.2.cloned.1.call-start = ((), (), s32[]{:S(2)}) async-start(), calls=%async_computation | async-start | bytes 1048576 | tf_op jit(solution)/shard_map/while/body/eval_jaxpr/psum | solution.py:29
  1209.8 7.6 copy-start
  1218.9 14.2 %collective-permute-start = (f32[2048,128]{0,1:T(8,128)S(1)}, f32[2048,128]{0,1:T(8,128)S(1)}, u32[]{:S(2)}, u32[]{:S(2)}) collective-permute-start(f32[2048,128]{0,1:T(8,128)S(1)} %fusion.23), channel_id=1, source_target_pairs={{0,32},{32,64},{64,96},{96,128},{128,160},{160,192},{192,224},{224... | collective-permute-start | bytes 3145736 | tf_op jit(solution)/shard_map/while/body/eval_jaxpr/ppermute | solution.py:10
  1233.2 150.6 %all-reduce.2.cloned.1.call-start = ((), (), s32[]{:S(2)}) async-start(), calls=%async_computation | async-start | bytes 1048576 | tf_op jit(solution)/shard_map/while/body/eval_jaxpr/psum | solution.py:29
  1383.8 7.6 copy-start
  1392.9 14.2 %collective-permute-start = (f32[2048,128]{0,1:T(8,128)S(1)}, f32[2048,128]{0,1:T(8,128)S(1)}, u32[]{:S(2)}, u32[]{:S(2)}) collective-permute-start(f32[2048,128]{0,1:T(8,128)S(1)} %fusion.23), channel_id=1, source_target_pairs={{0,32},{32,64},{64,96},{96,128},{128,160},{160,192},{192,224},{224... | collective-permute-start | bytes 3145736 | tf_op jit(solution)/shard_map/while/body/eval_jaxpr/ppermute | solution.py:10
Sparse Core Ops, SparseCore 0:
  15.1 151.8 all-reduce.1
  195.1 145.7 all-reduce.1
  369.0 145.7 all-reduce.1
  542.7 145.7 all-reduce.1
  716.3 145.7 all-reduce.1
  890.0 145.7 all-reduce.1
  1064.0 145.7 all-reduce.1
  1238.0 145.7 all-reduce.1
where the time goes:
time: 1420 us
  waiting for transfers between devices  1290 us (91%)
  matrix products  102 us (7%)
    psum x8, waiting for transfers between devices, advance(): summed_term = lax.psum(partial_value, 'rows')  1180 us
    ppermute x8, waiting for transfers between devices, from_behind(): return lax.ppermute(value, axis, pairs)  114 us
    dot_general x8, matrix products, advance(): lax.dot_general(summed_term, inverse_grams, contract_cols, precision=lax....  60.7 us
    dot_general x8, matrix products, advance(): lax.dot_general(rounded, features, contract_rows, preferred_element_type=...  29.6 us
  transfers between devices with their start and end apart: 16, of which 16 were waited for; matrix products, arithmetic and copies ran while one was open for 0% of the time, Pallas kernels for 0%

commit v1 on v0

v1 whole, which is shorter than its diff:
```python
import functools

import jax
import jax.numpy as jnp
from jax import lax
from jax.experimental import pallas as pl
from jax.experimental.pallas import tpu as pltpu
from jax.sharding import PartitionSpec as P

NY = 4
CHAINS = 2
PIECES = 2
TILE = 256
MESH = pl.DeviceIdType.MESH
BF16, F32 = jnp.bfloat16, jnp.float32
NT = (((1,), (1,)), ((), ()))


def wait_for(ref, sem):
    pltpu.make_async_copy(ref, ref, sem).wait()


def sweep(nf, nz, x_hbm, r_hbm, h_hbm, inc_hbm, res_hbm, xv, yv, hst, hsp, rst, fin, inb, outb,
          acc, q, rb, yb, uall, x_in, h_in, r_in, x_recv, x_send, z_recv, z_send, y_recv, y_send,
          g_recv, g_send, out_sem):
    rows, fb = xv.shape
    width = acc.shape[1]
    cw = fb // nz
    kc = rows // PIECES
    visits = nf
    f = lax.axis_index("feat")
    rid = lax.axis_index("rows")
    z, y = rid // NY, rid % NY
    nxt, prv = (f + 1) % nf, (f + nf - 1) % nf

    def at_z(d):
        return {"rows": ((z + d) % nz) * NY + y}

    def at_y(d):
        return {"rows": z * NY + (y + d) % NY}

    z_order = sorted(range(1, nz), key=lambda d: -min(d, nz - d))
    x_blocks = rows // TILE

    def load_x(t):
        part = pl.ds(t * TILE, TILE)
        return pltpu.make_async_copy(x_hbm.at[part], xv.at[part], x_in.at[t])

    pltpu.make_async_copy(h_hbm, hst, h_in).start()
    pltpu.make_async_copy(r_hbm, rst, r_in).start()
    for t in range(x_blocks):
        load_x(t).start()

    barrier = pltpu.get_barrier_semaphore()
    for peer in [at_z(d) for d in range(1, nz)] + [at_y(d) for d in range(1, NY)] + [{"feat": nxt}, {"feat": prv}]:
        pl.semaphore_signal(barrier, inc=1, device_id=peer, device_id_type=MESH)

    pltpu.make_async_copy(h_hbm, hst, h_in).wait()

    @pl.loop(0, fb // 128)
    def _(i):
        part = pl.ds(pl.multiple_of(i * 128, 128), 128)
        value = hst[part, :]
        high = value.astype(BF16)
        hsp[0, part, :] = high
        hsp[1, part, :] = (value - high.astype(F32)).astype(BF16)

    pltpu.make_async_copy(r_hbm, rst, r_in).wait()

    @pl.loop(0, rows // 128)
    def _(i):
        part = pl.ds(pl.multiple_of(i * 128, 128), 128)
        value = rst[part, :].T
        high = value.astype(BF16)
        low = (value - high.astype(F32)).astype(BF16)
        for s in range(CHAINS):
            own = slice(s * width, (s + 1) * width)
            inb[0, s, 0, :, part] = high[own]
            inb[0, s, 1, :, part] = low[own]

    @pl.loop(0, x_blocks)
    def _(t):
        part = pl.ds(pl.multiple_of(t * TILE, TILE), TILE)
        pltpu.make_async_copy(x_hbm.at[part], xv.at[part], x_in.at[t]).wait()
        block = xv[part, :]
        for n in range(fb // TILE):
            cols = slice(n * TILE, (n + 1) * TILE)
            value = jnp.dot(block, hsp[0, :, cols], preferred_element_type=F32)
            value += jnp.dot(block, hsp[1, :, cols], preferred_element_type=F32)
            yv[part, cols] = value.astype(BF16)

    pl.semaphore_wait(barrier, nz - 1 + NY - 1 + 2)

    def project(v, s):
        for c in range(PIECES):
            part = slice(c * kc, (c + 1) * kc)

            @pl.when(v > 0)
            def _():
                wait_for(inb.at[v, s, 0, :, part], x_recv.at[v, s, c])

            high = inb[v, s, 0, :, part]
            for n in range(fb // TILE):
                cols = slice(n * TILE, (n + 1) * TILE)
                value = jnp.dot(high, yv[part, cols], preferred_element_type=F32)
                if c > 0:
                    value += acc[s, :, cols]
                if c < PIECES - 1:
                    acc[s, :, cols] = value
                else:
                    for i in range(TILE // cw):
                        q[s, n * (TILE // cw) + i] = value[:, i * cw:(i + 1) * cw].astype(BF16)
        for d in z_order:
            pltpu.make_async_remote_copy(
                q.at[s, (z + d) % nz], rb.at[v, s, d - 1], z_send.at[s], z_recv.at[v, s],
                device_id=at_z(d), device_id_type=MESH).start()

    def reduce_z(v, s):
        wait_for(rb.at[v, s], z_recv.at[v, s])
        total = q[s, z].astype(F32)
        for d in range(1, nz):
            total += rb[v, s, d - 1].astype(F32)
        yb[v, s, y] = total
        wait_for(rb.at[v, s], z_send.at[s])
        for d in (2, 1, 3):
            pltpu.make_async_remote_copy(
                yb.at[v, s, y], yb.at[v, s, y], y_send.at[s], y_recv.at[v, s],
                device_id=at_y(d), device_id_type=MESH).start()

    def reduce_y(v, s):
        wait_for(yb.at[v, s, pl.ds(0, NY - 1)], y_recv.at[v, s])
        wait_for(yb.at[v, s, pl.ds(0, NY - 1)], y_send.at[s])
        total = yb[v, s, 0] + yb[v, s, 1] + yb[v, s, 2] + yb[v, s, 3]
        front = (f - v + nf) % nf
        cols = pl.ds(pl.multiple_of(z * cw, cw), cw)
        row = front * CHAINS + s
        uall[row, :, cols] = total.astype(BF16)
        for d in z_order:
            pltpu.make_async_remote_copy(
                uall.at[row, :, cols], uall.at[row, :, cols], g_send.at[s], g_recv.at[v, s],
                device_id=at_z(d), device_id_type=MESH).start()

    def apply(v, s):
        front = (f - v + nf) % nf
        row = front * CHAINS + s
        wait_for(rb.at[v, s], g_recv.at[v, s])
        wait_for(rb.at[v, s], g_send.at[s])

        @pl.when(v > 0)
        def _():
            wait_for(inb.at[v, s, 1], x_recv.at[v, s, PIECES])
            wait_for(outb.at[s], x_send.at[s])

        for c in range(PIECES):
            for t in range(c * kc // TILE, (c + 1) * kc // TILE):
                part = slice(t * TILE, (t + 1) * TILE)
                value = lax.dot_general(uall[row], xv[part, :], NT, preferred_element_type=F32)
                value = inb[v, s, 0, :, part].astype(F32) + inb[v, s, 1, :, part].astype(F32) - value
                high = value.astype(BF16)
                outb[s, 0, :, part] = high
                outb[s, 1, :, part] = (value - high.astype(F32)).astype(BF16)
            part = slice(c * kc, (c + 1) * kc)
            pltpu.make_async_remote_copy(
                outb.at[s, 0, :, part], inb.at[v + 1, s, 0, :, part], x_send.at[s],
                x_recv.at[v + 1, s, c], device_id={"feat": nxt}, device_id_type=MESH).start()
        pltpu.make_async_remote_copy(
            outb.at[s, 1], inb.at[v + 1, s, 1], x_send.at[s],
            x_recv.at[v + 1, s, PIECES], device_id={"feat": nxt}, device_id_type=MESH).start()

    @pl.loop(0, visits)
    def _(v):
        project(v, 0)

        @pl.when(v > 0)
        def _():
            reduce_y(v - 1, 1)

        reduce_z(v, 0)

        @pl.when(v > 0)
        def _():
            apply(v - 1, 1)

        reduce_y(v, 0)
        project(v, 1)
        apply(v, 0)
        reduce_z(v, 1)

    reduce_y(visits - 1, 1)
    apply(visits - 1, 1)

    incs = pltpu.make_async_copy(uall, inc_hbm, out_sem.at[0])
    incs.start()
    for s in range(CHAINS):
        for c in range(PIECES):
            part = slice(c * kc, (c + 1) * kc)
            wait_for(inb.at[visits, s, 0, :, part], x_recv.at[visits, s, c])
        wait_for(inb.at[visits, s, 1], x_recv.at[visits, s, PIECES])

        @pl.loop(0, rows // 128)
        def _(i):
            part = pl.ds(pl.multiple_of(i * 128, 128), 128)
            value = inb[visits, s, 0, :, part].astype(F32) + inb[visits, s, 1, :, part].astype(F32)
            fin[s * width:(s + 1) * width, part] = value

    final = pltpu.make_async_copy(fin, res_hbm, out_sem.at[1])
    final.start()
    for s in range(CHAINS):
        wait_for(outb.at[s], x_send.at[s])
    incs.wait()
    final.wait()


def on_device(nf, nr, features, residual, inverse_grams):
    rows, fb = features.shape
    labels = residual.shape[1]
    nz = nr // NY
    width = labels // CHAINS
    cw = fb // nz
    dma = pltpu.SemaphoreType.DMA
    hbm = pl.BlockSpec(memory_space=pl.ANY)
    increments, final = pl.pallas_call(
        functools.partial(sweep, nf, nz),
        out_shape=(
            jax.ShapeDtypeStruct((nf * CHAINS, width, fb), BF16),
            jax.ShapeDtypeStruct((labels, rows), F32),
        ),
        in_specs=[hbm, hbm, hbm],
        out_specs=(hbm, hbm),
        scratch_shapes=[
            pltpu.VMEM((rows, fb), BF16),
            pltpu.VMEM((rows, fb), BF16),
            pltpu.VMEM((fb, fb), F32),
            pltpu.VMEM((2, fb, fb), BF16),
            pltpu.VMEM((rows, labels), F32),
            pltpu.VMEM((labels, rows), F32),
            pltpu.VMEM((nf + 1, CHAINS, 2, width, rows), BF16),
            pltpu.VMEM((CHAINS, 2, width, rows), BF16),
            pltpu.VMEM((CHAINS, width, fb), F32),
            pltpu.VMEM((CHAINS, nz, width, cw), BF16),
            pltpu.VMEM((nf, CHAINS, nz - 1, width, cw), BF16),
            pltpu.VMEM((nf, CHAINS, NY, width, cw), F32),
            pltpu.VMEM((nf * CHAINS, width, fb), BF16),
            dma((rows // TILE,)),
            dma,
            dma,
            dma((nf + 1, CHAINS, PIECES + 1)),
            dma((CHAINS,)),
            dma((nf, CHAINS)),
            dma((CHAINS,)),
            dma((nf, CHAINS)),
            dma((CHAINS,)),
            dma((nf, CHAINS)),
            dma((CHAINS,)),
            dma((2,)),
        ],
        compiler_params=pltpu.CompilerParams(
            collective_id=0, has_side_effects=True, vmem_limit_bytes=60 * 1024 * 1024
        ),
        name="sweep",
    )(features, residual, inverse_grams)
    return increments.reshape(nf * labels, fb), final.T


def solution(mesh):
    placed = (P("rows", "feat"), P("rows", "feat"), P("feat", None))
    return jax.shard_map(
        functools.partial(on_device, mesh.shape["feat"], mesh.shape["rows"]),
        mesh=mesh,
        in_specs=placed,
        out_specs=(P(None, "feat"), P("rows", "feat")),
        check_vma=False,
    )
```

time: 1420 us -> 200 us (0.14)
  waiting for transfers between devices: 1290 us -> 0 us
  Pallas kernels: 0 us -> 194 us
  matrix products: 102 us -> 0 us
    psum x8 -> x0, waiting for transfers between devices: 1180 us -> none  [advance(): summed_term = lax.psum(partial_value, 'rows')]
    pallas_call x0 -> x1, Pallas kernels: none -> 194 us  [on_device(): pl.pallas_call(functools.partial(sweep, nf, nz), out_shape=(jax.ShapeDtyp...]
    ppermute x8 -> x0, waiting for transfers between devices: 114 us -> none  [from_behind(): return lax.ppermute(value, axis, pairs)]
    dot_general x24 -> x0, matrix products: 102 us -> none  [the longest x8 60.7 us: advance(): lax.dot_general(summed_term, inverse_grams, contract_cols, precision=lax....]
  transfers between devices with their start and end apart: 16 -> 0, of which waited for: 16 -> 0; matrix products, arithmetic and copies ran while one was open for 0% -> 0% of each run, Pallas kernels for 0% -> 0%
where the time goes in v1:
time: 200 us
  Pallas kernels  194 us (97%)
  local copies, waits for them, and re-layouts  5.61 us (3%)
    pallas_call x1, Pallas kernels, on_device(): pl.pallas_call(functools.partial(sweep, nf, nz), out_shape=(jax.ShapeDtyp...  194 us
    unnamed x2, local copies, waits for them, and re-layouts  5.61 us

profile of v1, /device:TPU:2, one launch (start us, length us, event | category | flops | bytes accessed | tf_op | source)
XLA Modules:
  0.0 200.2 jit_solution(4818330636974421355)
XLA Ops:
  0.6 194.0 %sweep.1 = (bf16[16,64,1024]{2,1,0:T(8,128)(2,1)}, f32[128,2048]{1,0:T(8,128)}) custom-call(bf16[2048,1024]{1,0:T(8,128)(2,1)} %x_hbm.1, f32[2048,128]{1,0:T(8,128)} %r_hbm.1, f32[1024,1024]{1,0:T(8,128)} %h_hbm.1), custom_call_target="tpu_custom_call" | custom-call | tf_op jit(solution)/shard_map/sweep/pallas_call | solution.py:222
  194.6 2.5 %copy.5 = f32[2048,128]{1,0:T(8,128)} copy(f32[2048,128]{0,1:T(8,128)} %bitcast.3) | data formatting | bytes 2097152
  197.1 3.1 %copy.7 = bf16[1024,1024]{1,0:T(8,128)(2,1)} copy(bf16[1024,1024]{1,0:T(8,128)(2,1)} %bitcast.2) | data formatting | bytes 4194304

commit v2 on v1

v2 whole, which is shorter than its diff:
```python
import functools

import jax
import jax.numpy as jnp
from jax import lax
from jax.experimental import pallas as pl
from jax.experimental.pallas import tpu as pltpu
from jax.sharding import PartitionSpec as P

NY = 4
SCHEDULE = ("P0", "A1-", "L1-", "U0", "P1", "A0", "L0", "U1")
CHAINS = 2
PIECES = 2
TILE = 256
MESH = pl.DeviceIdType.MESH
BF16, F32 = jnp.bfloat16, jnp.float32
NT = (((1,), (1,)), ((), ()))


def wait_for(ref, sem):
    pltpu.make_async_copy(ref, ref, sem).wait()


def sweep(nf, nz, x_hbm, r_hbm, h_hbm, uall, fin, xv, xt, yv, hst, hsp, rst, inb, home, outb,
          acc, q, pv, rb, x_in, h_in, r_in, x_recv, x_send, e_send, q_recv, q_send,
          g_recv, g_send):
    rows, fb = xv.shape
    width = acc.shape[1]
    sw, cw = q.shape[3], q.shape[4]
    kc = rows // PIECES
    visits = nf
    f = lax.axis_index("feat")
    rid = lax.axis_index("rows")
    z, y = rid // NY, rid % NY
    nxt, prv = (f + 1) % nf, (f + nf - 1) % nf
    x_blocks = rows // TILE
    my_rows = pl.ds(pl.multiple_of(y * sw, sw), sw)
    my_cols = pl.ds(pl.multiple_of(z * cw, cw), cw)

    peers = [(dz, dy) for dz in range(nz) for dy in range(NY) if dz or dy]
    peers.sort(key=lambda p: -(min(p[0], nz - p[0]) + min(p[1], NY - p[1])))

    def place(dz, dy):
        return (z + dz) % nz, (y + dy) % NY

    def device(pz, py):
        return {"rows": pz * NY + py}

    def load_x(t):
        part = pl.ds(t * TILE, TILE)
        return pltpu.make_async_copy(x_hbm.at[part], xv.at[part], x_in.at[t])

    pltpu.make_async_copy(r_hbm, rst, r_in).start()
    for t in range(x_blocks):
        load_x(t).start()
    pltpu.make_async_copy(h_hbm, hst, h_in).start()

    barrier = pltpu.get_barrier_semaphore()
    for peer in [device(*place(*p)) for p in peers] + [{"feat": nxt}, {"feat": prv}]:
        pl.semaphore_signal(barrier, inc=1, device_id=peer, device_id_type=MESH)

    pltpu.make_async_copy(r_hbm, rst, r_in).wait()

    @pl.loop(0, rows // 128)
    def _(i):
        part = pl.ds(pl.multiple_of(i * 128, 128), 128)
        value = rst[part, :].T
        high = value.astype(BF16)
        low = (value - high.astype(F32)).astype(BF16)
        for s in range(CHAINS):
            own = slice(s * width, (s + 1) * width)
            inb[0, s, 0, :, part] = high[own]
            inb[0, s, 1, :, part] = low[own]

    for t in range(x_blocks):
        load_x(t).wait()

    def split_inverse():
        pltpu.make_async_copy(h_hbm, hst, h_in).wait()

        @pl.loop(0, fb // 128)
        def _(i):
            part = pl.ds(pl.multiple_of(i * 128, 128), 128)
            value = hst[part, :]
            high = value.astype(BF16)
            hsp[0, part, :] = high
            hsp[1, part, :] = (value - high.astype(F32)).astype(BF16)

    def times_inverse(value, cols):
        high = jnp.dot(value, hsp[0, :, cols], preferred_element_type=F32)
        return high + jnp.dot(value, hsp[1, :, cols], preferred_element_type=F32)

    def form_y(first, last):
        @pl.loop(first, last)
        def _(t):
            part = pl.ds(pl.multiple_of(t * TILE, TILE), TILE)
            block = xv[part, :]
            for n in range(fb // TILE):
                cols = slice(n * TILE, (n + 1) * TILE)
                yv[part, cols] = times_inverse(block, cols).astype(BF16)

    def project(v, s, start=False):
        for c in range(PIECES):
            part = slice(c * kc, (c + 1) * kc)
            if not start:
                wait_for(inb.at[v, s, 0, :, part], x_recv.at[v, s, c])
            high = inb[v, s, 0, :, part]
            for n in range(fb // TILE):
                cols = slice(n * TILE, (n + 1) * TILE)
                value = jnp.dot(high, (xv if start else yv)[part, cols], preferred_element_type=F32)
                if c > 0:
                    value += acc[s, :, cols]
                if c < PIECES - 1:
                    acc[s, :, cols] = value
                else:
                    for i in range(TILE // cw):
                        for j in range(NY):
                            q[s, j, n * (TILE // cw) + i] = value[j * sw:(j + 1) * sw, i * cw:(i + 1) * cw].astype(BF16)
        for i, p in enumerate(peers):
            pz, py = place(*p)
            pltpu.make_async_remote_copy(
                q.at[s, py, pz], rb.at[v, s, i], q_send.at[s], q_recv.at[v, s],
                device_id=device(pz, py), device_id_type=MESH).start()

    def reduce(v, s, start=False):
        wait_for(rb.at[v, s], q_recv.at[v, s])
        total = q[s, y, z].astype(F32)
        for i in range(len(peers)):
            total += rb[v, s, i].astype(F32)
        row = (f - v + nf) % nf * CHAINS + s
        target = pv.at[s] if start else uall.at[row]
        target[my_rows, my_cols] = total.astype(BF16)
        for p in peers:
            pltpu.make_async_remote_copy(
                target.at[my_rows, my_cols], target.at[my_rows, my_cols], g_send.at[s], g_recv.at[v, s],
                device_id=device(*place(*p)), device_id_type=MESH).start()
        wait_for(rb.at[v, s], q_send.at[s])

    def apply(v, s, start=False, last=False):
        row = (f - v + nf) % nf * CHAINS + s
        wait_for(rb.at[v, s], g_recv.at[v, s])
        if start:
            for n in range(fb // TILE):
                cols = slice(n * TILE, (n + 1) * TILE)
                uall[row, :, cols] = times_inverse(pv[s], cols).astype(BF16)
        else:
            if not last:
                wait_for(inb.at[v, s, 1], x_recv.at[v, s, PIECES])
            wait_for(outb.at[s], x_send.at[s])
        for c in range(PIECES):
            for t in range(c * kc // TILE, (c + 1) * kc // TILE):
                part = slice(t * TILE, (t + 1) * TILE)
                if start:
                    value = lax.dot_general(uall[row], xv[part, :], NT, preferred_element_type=F32)
                else:
                    value = jnp.dot(uall[row], xt[:, part], preferred_element_type=F32)
                if last:
                    outb[s, 0, :, part] = value.astype(BF16)
                    continue
                value = inb[v, s, 0, :, part].astype(F32) + inb[v, s, 1, :, part].astype(F32) - value
                high = value.astype(BF16)
                outb[s, 0, :, part] = high
                outb[s, 1, :, part] = (value - high.astype(F32)).astype(BF16)
            part = slice(c * kc, (c + 1) * kc)
            pltpu.make_async_remote_copy(
                outb.at[s, 0, :, part], home.at[s, :, part] if last else inb.at[v + 1, s, 0, :, part], x_send.at[s],
                x_recv.at[v + (2 if last else 1), s, c], device_id={"feat": nxt}, device_id_type=MESH).start()
        wait_for(rb.at[v, s], g_send.at[s])

    def send_low(v, s):
        pltpu.make_async_remote_copy(
            outb.at[s, 1], inb.at[v + 1, s, 1], x_send.at[s],
            x_recv.at[v + 1, s, PIECES], device_id={"feat": nxt}, device_id_type=MESH).start()

    def forward(v, s, i):
        if i == 1:
            wait_for(inb.at[v, s, 1], x_recv.at[v, s, PIECES])
        return pltpu.make_async_remote_copy(
            inb.at[v, s, i], inb.at[v + 1, s, i], e_send.at[s, i],
            x_recv.at[v + 1, s, PIECES if i else 0], device_id={"feat": nxt}, device_id_type=MESH)

    pl.semaphore_wait(barrier, len(peers) + 2)
    for s in range(CHAINS):
        project(0, s, True)
    split_inverse()
    form_y(0, x_blocks // 2)
    for s in range(CHAINS):
        reduce(0, s, True)
    form_y(x_blocks // 2, x_blocks)
    for s in range(CHAINS):
        apply(0, s, True)
    for s in range(CHAINS):
        send_low(0, s)

    @pl.loop(0, rows // 128)
    def _(i):
        part = pl.ds(pl.multiple_of(i * 128, 128), 128)
        xt[:, part] = xv[part, :].T

    stages = {"P": project, "U": reduce, "A": apply, "L": send_low}
    steps = [(stages[w[0]], int(w[1]), len(w) > 2) for w in SCHEDULE]

    @pl.loop(1, visits - 1)
    def _(v):
        for stage, s, late in steps:
            if late:
                @pl.when(v > 1)
                def _():
                    stage(v - 1, s)
            else:
                stage(v, s)

    end = visits - 1
    for stage, s, late in steps:
        if late:
            if end > 1:
                stage(end - 1, s)
            continue
        if stage is send_low:
            continue
        if stage is apply:
            apply(end, s, last=True)
            continue
        stage(end, s)
        if stage is project:
            forward(end, s, 0).start()
        if stage is reduce:
            forward(end, s, 1).start()
    for stage, s, late in steps:
        if late and stage is apply:
            apply(end, s, last=True)

    for s in range(CHAINS):
        wait_for(inb.at[visits, s, 0], x_recv.at[visits, s, 0])
        wait_for(inb.at[visits, s, 1], x_recv.at[visits, s, PIECES])
        for c in range(PIECES):
            part = slice(c * kc, (c + 1) * kc)
            wait_for(home.at[s, :, part], x_recv.at[visits + 1, s, c])

            @pl.loop(c * kc // 128, (c + 1) * kc // 128)
            def _(i):
                part = pl.ds(pl.multiple_of(i * 128, 128), 128)
                value = inb[visits, s, 0, :, part].astype(F32) + inb[visits, s, 1, :, part].astype(F32)
                fin[part, s * width:(s + 1) * width] = (value - home[s, :, part].astype(F32)).T

    for s in range(CHAINS):
        wait_for(inb.at[visits, s, 0], e_send.at[s, 0])
        wait_for(inb.at[visits, s, 1], e_send.at[s, 1])
        wait_for(outb.at[s, 0], x_send.at[s])


def on_device(nf, nr, features, residual, inverse_grams):
    rows, fb = features.shape
    labels = residual.shape[1]
    nz = nr // NY
    width = labels // CHAINS
    cw, sw = fb // nz, width // NY
    dma = pltpu.SemaphoreType.DMA
    hbm = pl.BlockSpec(memory_space=pltpu.HBM)
    vmem = pl.BlockSpec(memory_space=pltpu.VMEM)
    increments, final = pl.pallas_call(
        functools.partial(sweep, nf, nz),
        out_shape=(
            pltpu.VMEM((nf * CHAINS, width, fb), BF16),
            pltpu.VMEM((rows, labels), F32),
        ),
        in_specs=[hbm, hbm, hbm],
        out_specs=(vmem, vmem),
        scratch_shapes=[
            pltpu.VMEM((rows, fb), BF16),
            pltpu.VMEM((fb, rows), BF16),
            pltpu.VMEM((rows, fb), BF16),
            pltpu.VMEM((fb, fb), F32),
            pltpu.VMEM((2, fb, fb), BF16),
            pltpu.VMEM((rows, labels), F32),
            pltpu.VMEM((nf + 1, CHAINS, 2, width, rows), BF16),
            pltpu.VMEM((CHAINS, width, rows), BF16),
            pltpu.VMEM((CHAINS, 2, width, rows), BF16),
            pltpu.VMEM((CHAINS, width, fb), F32),
            pltpu.VMEM((CHAINS, NY, nz, sw, cw), BF16),
            pltpu.VMEM((CHAINS, width, fb), BF16),
            pltpu.VMEM((nf, CHAINS, nr - 1, sw, cw), BF16),
            dma((rows // TILE,)),
            dma,
            dma,
            dma((nf + 2, CHAINS, PIECES + 1)),
            dma((CHAINS,)),
            dma((CHAINS, 2)),
            dma((nf, CHAINS)),
            dma((CHAINS,)),
            dma((nf, CHAINS)),
            dma((CHAINS,)),
        ],
        compiler_params=pltpu.CompilerParams(
            collective_id=0, has_side_effects=True, vmem_limit_bytes=60 * 1024 * 1024
        ),
        name="sweep",
    )(features, residual, inverse_grams)
    return increments.reshape(nf * labels, fb), final


def solution(mesh):
    placed = (P("rows", "feat"), P("rows", "feat"), P("feat", None))
    return jax.shard_map(
        functools.partial(on_device, mesh.shape["feat"], mesh.shape["rows"]),
        mesh=mesh,
        in_specs=placed,
        out_specs=(P(None, "feat"), P("rows", "feat")),
        check_vma=False,
    )
```

time: 200 us -> 165 us (0.82)
  Pallas kernels: 194 us -> 162 us
  local copies, waits for them, and re-layouts: 5.61 us -> 2.29 us
    pallas_call x1, Pallas kernels: 194 us -> 162 us  [on_device(): pl.pallas_call(functools.partial(sweep, nf, nz), out_shape=(pltpu.VMEM((n...]
    unnamed x2, local copies, waits for them, and re-layouts: 5.61 us -> 2.29 us
where the time goes in v2:
time: 165 us
  Pallas kernels  162 us (98%)
  local copies, waits for them, and re-layouts  2.29 us (1%)
    pallas_call x1, Pallas kernels, on_device(): pl.pallas_call(functools.partial(sweep, nf, nz), out_shape=(pltpu.VMEM((n...  162 us

profile of v2, /device:TPU:2, one launch (start us, length us, event | category | flops | bytes accessed | tf_op | source)
XLA Modules:
  0.0 165.1 jit_solution(11380393806927464688)
XLA Ops:
  0.6 162.2 %sweep.1 = (bf16[16,64,1024]{2,1,0:T(8,128)(2,1)S(1)}, f32[2048,128]{1,0:T(8,128)S(1)}) custom-call(bf16[2048,1024]{1,0:T(8,128)(2,1)} %x_hbm.1, f32[2048,128]{1,0:T(8,128)} %r_hbm.1, f32[1024,1024]{1,0:T(8,128)} %h_hbm.1), custom_call_target="tpu_custom_call" | custom-call | tf_op jit(solution)/shard_map/sweep/pallas_call | solution.py:261
  162.8 1.3 copy.7
  164.2 1.0 copy.8

commit v3 on v2

--- a/solution.py
+++ b/solution.py
@@ -8,7 +8,7 @@
 from jax.sharding import PartitionSpec as P
 
 NY = 4
-SCHEDULE = ("P0", "A1-", "L1-", "U0", "P1", "A0", "L0", "U1")
+SCHEDULE = ("P0", "P1", "U0", "U1", "A0", "A1", "L0", "L1")
 CHAINS = 2
 PIECES = 2
 TILE = 256
@@ -116,6 +116,8 @@
                     for i in range(TILE // cw):
                         for j in range(NY):
                             q[s, j, n * (TILE // cw) + i] = value[j * sw:(j + 1) * sw, i * cw:(i + 1) * cw].astype(BF16)
+        if start and s == 0:
+            pl.semaphore_wait(barrier, len(peers) + 2)
         for i, p in enumerate(peers):
             pz, py = place(*p)
             pltpu.make_async_remote_copy(
@@ -172,6 +174,12 @@
             outb.at[s, 1], inb.at[v + 1, s, 1], x_send.at[s],
             x_recv.at[v + 1, s, PIECES], device_id={"feat": nxt}, device_id_type=MESH).start()
 
+    def transpose_x():
+        @pl.loop(0, rows // 128)
+        def _(i):
+            part = pl.ds(pl.multiple_of(i * 128, 128), 128)
+            xt[:, part] = xv[part, :].T
+
     def forward(v, s, i):
         if i == 1:
             wait_for(inb.at[v, s, 1], x_recv.at[v, s, PIECES])
@@ -179,7 +187,6 @@
             inb.at[v, s, i], inb.at[v + 1, s, i], e_send.at[s, i],
             x_recv.at[v + 1, s, PIECES if i else 0], device_id={"feat": nxt}, device_id_type=MESH)
 
-    pl.semaphore_wait(barrier, len(peers) + 2)
     for s in range(CHAINS):
         project(0, s, True)
     split_inverse()
@@ -192,17 +199,16 @@
     for s in range(CHAINS):
         send_low(0, s)
 
-    @pl.loop(0, rows // 128)
-    def _(i):
-        part = pl.ds(pl.multiple_of(i * 128, 128), 128)
-        xt[:, part] = xv[part, :].T
-
     stages = {"P": project, "U": reduce, "A": apply, "L": send_low}
     steps = [(stages[w[0]], int(w[1]), len(w) > 2) for w in SCHEDULE]
 
+    middle = [late or stage is not reduce for stage, _, late in steps].index(False)
+
     @pl.loop(1, visits - 1)
     def _(v):
-        for stage, s, late in steps:
+        for at, (stage, s, late) in enumerate(steps):
+            if at == middle:
+                pl.when(v == 1)(transpose_x)
             if late:
                 @pl.when(v > 1)
                 def _():
@@ -211,6 +217,8 @@
                 stage(v, s)
 
     end = visits - 1
+    if end == 1:
+        transpose_x()
     for stage, s, late in steps:
         if late:
             if end > 1:
@@ -226,11 +234,7 @@
             forward(end, s, 0).start()
         if stage is reduce:
             forward(end, s, 1).start()
-    for stage, s, late in steps:
-        if late and stage is apply:
-            apply(end, s, last=True)
-
-    for s in range(CHAINS):
+    def finish(s):
         wait_for(inb.at[visits, s, 0], x_recv.at[visits, s, 0])
         wait_for(inb.at[visits, s, 1], x_recv.at[visits, s, PIECES])
         for c in range(PIECES):
@@ -242,6 +246,21 @@
                 part = pl.ds(pl.multiple_of(i * 128, 128), 128)
                 value = inb[visits, s, 0, :, part].astype(F32) + inb[visits, s, 1, :, part].astype(F32)
                 fin[part, s * width:(s + 1) * width] = (value - home[s, :, part].astype(F32)).T
+
+    done = []
+    for stage, s, late in steps:
+        if not late or stage is send_low:
+            continue
+        if stage is apply:
+            finish(s - 1)
+            done.append(s - 1)
+            apply(end, s, last=True)
+        else:
+            stage(end, s)
+            forward(end, s, 1).start()
+    for s in range(CHAINS):
+        if s not in done:
+            finish(s)
 
     for s in range(CHAINS):
         wait_for(inb.at[visits, s, 0], e_send.at[s, 0])

time: 165 us -> 163 us (0.988)
  Pallas kernels: 162 us -> 160 us
    pallas_call x1, Pallas kernels: 162 us -> 160 us  [on_device(): pl.pallas_call(functools.partial(sweep, nf, nz), out_shape=(pltpu.VMEM((n...]
where the time goes in v3:
time: 163 us
  Pallas kernels  160 us (98%)
  local copies, waits for them, and re-layouts  2.29 us (1%)
    pallas_call x1, Pallas kernels, on_device(): pl.pallas_call(functools.partial(sweep, nf, nz), out_shape=(pltpu.VMEM((n...  160 us

profile of v3, /device:TPU:2, one launch (start us, length us, event | category | flops | bytes accessed | tf_op | source)
XLA Modules:
  0.0 163.1 jit_solution(7179390373832821248)
XLA Ops:
  0.6 160.2 %sweep.1 = (bf16[16,64,1024]{2,1,0:T(8,128)(2,1)S(1)}, f32[2048,128]{1,0:T(8,128)S(1)}) custom-call(bf16[2048,1024]{1,0:T(8,128)(2,1)} %x_hbm.1, f32[2048,128]{1,0:T(8,128)} %r_hbm.1, f32[1024,1024]{1,0:T(8,128)} %h_hbm.1), custom_call_target="tpu_custom_call" | custom-call | tf_op jit(solution)/shard_map/sweep/pallas_call | solution.py:280
  160.8 1.3 copy.7
  162.1 1.0 copy.8

commit v4 on v3

--- a/solution.py
+++ b/solution.py
@@ -11,7 +11,7 @@
 SCHEDULE = ("P0", "P1", "U0", "U1", "A0", "A1", "L0", "L1")
 CHAINS = 2
 PIECES = 2
-TILE = 256
+TILE = 512
 MESH = pl.DeviceIdType.MESH
 BF16, F32 = jnp.bfloat16, jnp.float32
 NT = (((1,), (1,)), ((), ()))

time: 163 us -> 163 us (level)
  no operation moved by 1% of the time
where the time goes in v4:
time: 163 us; the launch traced here: 162 us
  Pallas kernels  159 us (98%)
  local copies, waits for them, and re-layouts  2.29 us (1%)
    pallas_call x1, Pallas kernels, on_device(): pl.pallas_call(functools.partial(sweep, nf, nz), out_shape=(pltpu.VMEM((n...  159 us

profile of v4, /device:TPU:2, one launch (start us, length us, event | category | flops | bytes accessed | tf_op | source)
XLA Modules:
  0.0 162.3 jit_solution(7545223897199712817)
XLA Ops:
  0.6 159.4 %sweep.1 = (bf16[16,64,1024]{2,1,0:T(8,128)(2,1)S(1)}, f32[2048,128]{1,0:T(8,128)S(1)}) custom-call(bf16[2048,1024]{1,0:T(8,128)(2,1)} %x_hbm.1, f32[2048,128]{1,0:T(8,128)} %r_hbm.1, f32[1024,1024]{1,0:T(8,128)} %h_hbm.1), custom_call_target="tpu_custom_call" | custom-call | tf_op jit(solution)/shard_map/sweep/pallas_call | solution.py:280
  160.1 1.3 copy.7
  161.4 1.0 copy.8
